TPU v7x, 32 devices: a whole 2x2x4 slice. The times are simulated.
32 devices in a mesh: groups: 2 (over x), track: 8 (over z, y), sub: 2 (over core).
Axes of the slice: x: 2, y: 2, z: 4, core: 2. Of those that a mesh axis runs over, the one named last changes fastest.
Arguments:
- tokens: bfloat16 [512, 128, 384], P(('groups', 'track', 'sub')), parts along dimension 0, may hold values from -6 to 6
- visible: int32 [512, 2], P(('groups', 'track', 'sub')), parts along dimension 0, may hold values from 0 to 128, as said below
- time_attn: bfloat16 [4, 384, 384], replicated, may hold values from -0.3125 to 0.3125
- mlp_in: bfloat16 [384, 1536], replicated, may hold values from -0.3125 to 0.3125
- mlp_out: bfloat16 [1536, 384], replicated, may hold values from -0.15625 to 0.15625
- virt_attn: bfloat16 [3, 4, 384, 384], replicated, may hold values from -0.3125 to 0.3125
- virtual: bfloat16 [64, 384], replicated, may hold values from -6 to 6
Outputs:
- updated: bfloat16 [512, 128, 384], P(('groups', 'track', 'sub')), parts along dimension 0
There are 2 independent parts, one for each index of `groups`. A program takes and returns all parts, laid end to end along the dimension named above; an argument that names none is the same for every part. Nothing has to cross between parts.
Inputs may be any that keep to these rules, and one draw needn't show every extreme that they name: visible[n, 0] < visible[n, 1]; the first track of every block of 16 tracks is visible in all 128 frames.
All inputs are finite; a program needn't handle non-finite values.
Results may differ from a plain program's by a relative error of at most 0.0095.
Values may be sent and summed in bfloat16 or wider, within the bound.
A program may use at most 128 MiB of HBM per device.

v0:
```python
import functools
import math

import jax
import jax.numpy as jnp
from jax import lax
from jax.experimental import pallas as pl
from jax.experimental.pallas import tpu as pltpu
from jax.sharding import PartitionSpec as P

HEADS = 8
F32 = jnp.float32
BF16 = jnp.bfloat16


def layer_norm(values):
    wide = values.astype(F32)
    center = wide - jnp.mean(wide, axis=-1, keepdims=True)
    spread = jnp.mean(center * center, axis=-1, keepdims=True)
    return (center * lax.rsqrt(spread + 1e-05)).astype(BF16)


def project(values, matrix):
    return jnp.dot(values, matrix, preferred_element_type=F32)


def product(left, right, left_dim, right_dim):
    dims = (((left_dim,), (right_dim,)), ((), ()))
    return lax.dot_general(left, right, dims, preferred_element_type=F32)


def head_masks(feature, kind):
    size = feature // HEADS
    lanes = lax.broadcasted_iota(jnp.int32, (1, feature), 1)
    return [
        jnp.where((lanes >= head * size) & (lanes < (head + 1) * size), 1.0, 0.0).astype(kind)
        for head in range(HEADS)
    ]


def spread_heads(rows, masks):
    return jnp.concatenate([rows * mask for mask in masks], axis=0)


def time_step(tokens, first_frame, end_frame, attn_ref, in_ref, out_ref, ones_ref):
    tracks, frames, feature = tokens.shape
    scale = 1.0 / math.sqrt(feature // HEADS)
    masks = head_masks(feature, BF16)
    wide = tokens.reshape(tracks * frames, feature).astype(F32)
    normed = layer_norm(wide)
    queries = project(normed, attn_ref[0]).astype(BF16)
    keys = project(normed, attn_ref[1]).astype(BF16)
    values = project(normed, attn_ref[2]).astype(BF16)
    lane = lax.broadcasted_iota(jnp.int32, (1, frames), 1)
    row = lax.broadcasted_iota(jnp.int32, (frames, feature), 0)
    mixed, vis = [], []
    for track in range(tracks):
        part = slice(track * frames, (track + 1) * frames)
        seen = (lane >= first_frame[track]) & (lane < end_frame[track])
        scores = product(queries[part], spread_heads(keys[part], masks), 1, 1)
        weights = []
        for head in range(HEADS):
            own = scores[:, head * frames : (head + 1) * frames] * scale
            own = jnp.where(seen, own, -1e30)
            top = jnp.max(own, axis=-1, keepdims=True)
            weights.append(jnp.exp(own - top).astype(BF16))
        weights = jnp.concatenate(weights, axis=1)
        summed = project(weights, spread_heads(values[part], masks))
        total = project(weights, ones_ref[...])
        mixed.append((summed / total).astype(BF16))
        shown = (row >= first_frame[track]) & (row < end_frame[track])
        vis.append(jnp.where(shown, 1.0, 0.0).astype(F32))
    mixed = jnp.concatenate(mixed, axis=0)
    vis = jnp.concatenate(vis, axis=0)
    first = wide + vis * project(mixed, attn_ref[3])
    hidden = jax.nn.gelu(project(layer_norm(first), in_ref[...]), approximate=True).astype(BF16)
    return first + vis * project(hidden, out_ref[...])


def fill_ones(ones_ref, feature):
    rows = ones_ref.shape[0] // HEADS
    for head, mask in enumerate(head_masks(feature, F32)):
        ones_ref[head * rows : (head + 1) * rows, :] = jnp.broadcast_to(mask, (rows, feature)).astype(BF16)


def few_queries(spread_queries, keys, values, masks):
    feature = keys.shape[1]
    scores = product(spread_queries, keys, 1, 1) * (1.0 / math.sqrt(feature // HEADS))
    top = jnp.max(scores, axis=-1, keepdims=True)
    weights = jnp.exp(scores - top)
    total = jnp.sum(weights, axis=-1, keepdims=True)
    summed = project(weights.astype(BF16), values) / total
    count = spread_queries.shape[0] // HEADS
    mixed = summed[:count] * masks[0]
    for head in range(1, HEADS):
        mixed = mixed + summed[head * count : (head + 1) * count] * masks[head]
    return mixed.astype(BF16)


def frame_step(framed, attn_ref, virtual_ref, query_ref, ones_ref):
    frames, tracks, feature = framed.shape
    n_virtual = virtual_ref.shape[0]
    scale = 1.0 / math.sqrt(feature // HEADS)
    masks = head_masks(feature, BF16)
    wide_masks = head_masks(feature, F32)
    wide = framed.reshape(frames * tracks, feature).astype(F32)
    normed = layer_norm(wide)
    key_c = project(normed, attn_ref[0, 1]).astype(BF16)
    value_c = project(normed, attn_ref[0, 2]).astype(BF16)
    query_b = project(normed, attn_ref[2, 0]).astype(BF16)
    track_part = [slice(f * tracks, (f + 1) * tracks) for f in range(frames)]
    virtual_part = [slice(f * n_virtual, (f + 1) * n_virtual) for f in range(frames)]
    cross = [few_queries(query_ref[...], key_c[part], value_c[part], wide_masks) for part in track_part]
    base = jnp.concatenate([virtual_ref[...].astype(F32)] * frames, axis=0)
    first = base + project(jnp.concatenate(cross, axis=0), attn_ref[0, 3])
    normed_w = layer_norm(first)
    query_s = project(normed_w, attn_ref[1, 0]).astype(BF16)
    key_s = project(normed_w, attn_ref[1, 1]).astype(BF16)
    value_s = project(normed_w, attn_ref[1, 2]).astype(BF16)
    among = [
        few_queries(spread_heads(query_s[part], masks), key_s[part], value_s[part], wide_masks)
        for part in virtual_part
    ]
    second = first + project(jnp.concatenate(among, axis=0), attn_ref[1, 3])
    normed_b = layer_norm(second)
    key_b = project(normed_b, attn_ref[2, 1]).astype(BF16)
    value_b = project(normed_b, attn_ref[2, 2]).astype(BF16)
    back = []
    for frame in range(frames):
        part = virtual_part[frame]
        scores = product(spread_heads(key_b[part], masks), query_b[track_part[frame]], 1, 1) * scale
        scores = scores.reshape(HEADS, n_virtual, tracks)
        top = jnp.max(scores, axis=1, keepdims=True)
        weights = jnp.exp(scores - top).astype(BF16).reshape(HEADS * n_virtual, tracks)
        summed = product(weights, spread_heads(value_b[part], masks), 0, 0)
        total = product(weights, ones_ref[...], 0, 0)
        back.append((summed / total).astype(BF16))
    return wide + project(jnp.concatenate(back, axis=0), attn_ref[2, 3])


def time_kernel(vis_ref, tok_ref, attn_ref, in_ref, out_ref, x_ref, ones_ref):
    step = pl.program_id(0)
    tracks, frames, feature = tok_ref.shape

    @pl.when(step == 0)
    def _():
        fill_ones(ones_ref, feature)

    begin = [vis_ref[step * tracks + i, 0] for i in range(tracks)]
    end = [vis_ref[step * tracks + i, 1] for i in range(tracks)]
    after = time_step(tok_ref[...], begin, end, attn_ref, in_ref, out_ref, ones_ref)
    x_ref[...] = after.astype(BF16).reshape(tracks, frames, feature)


def frame_kernel(x_ref, attn_ref, virtual_ref, y_ref, query_ref, ones_ref):
    frames, tracks, feature = x_ref.shape

    @pl.when(pl.program_id(0) == 0)
    def _():
        fill_ones(ones_ref, feature)
        query = project(layer_norm(virtual_ref[...]), attn_ref[0, 0]).astype(BF16)
        query_ref[...] = spread_heads(query, head_masks(feature, BF16))

    after = frame_step(x_ref[...], attn_ref, virtual_ref, query_ref, ones_ref)
    y_ref[...] = after.astype(BF16).reshape(frames, tracks, feature)


WHOLE = pl.BlockSpec(memory_space=pltpu.VMEM)
LIMIT = 60 * 1024 * 1024


def time_block(tokens, visible, time_attn, mlp_in, mlp_out, group):
    tracks, frames, feature = tokens.shape
    spec = pl.BlockSpec((group, frames, feature), lambda i: (i, 0, 0))
    return pl.pallas_call(
        time_kernel,
        grid=(tracks // group,),
        in_specs=[pl.BlockSpec(memory_space=pltpu.SMEM), spec, WHOLE, WHOLE, WHOLE],
        out_specs=spec,
        out_shape=jax.ShapeDtypeStruct(tokens.shape, BF16),
        scratch_shapes=[pltpu.VMEM((HEADS * frames, feature), BF16)],
        compiler_params=pltpu.CompilerParams(vmem_limit_bytes=LIMIT),
    )(visible, tokens, time_attn, mlp_in, mlp_out)


def frame_block(framed, virt_attn, virtual, group):
    frames, tracks, feature = framed.shape
    n_virtual = virtual.shape[0]
    spec = pl.BlockSpec((group, tracks, feature), lambda i: (i, 0, 0))
    return pl.pallas_call(
        frame_kernel,
        grid=(frames // group,),
        in_specs=[spec, WHOLE, WHOLE],
        out_specs=spec,
        out_shape=jax.ShapeDtypeStruct(framed.shape, BF16),
        scratch_shapes=[
            pltpu.VMEM((HEADS * n_virtual, feature), BF16),
            pltpu.VMEM((HEADS * n_virtual, feature), BF16),
        ],
        compiler_params=pltpu.CompilerParams(vmem_limit_bytes=LIMIT),
    )(framed, virt_attn, virtual)


def shards(tokens, visible, time_attn, mlp_in, mlp_out, virt_attn, virtual):
    after = time_block(tokens, visible, time_attn, mlp_in, mlp_out, 2)
    by_frame = lax.all_to_all(after, ("track", "sub"), split_axis=1, concat_axis=0, tiled=True)
    framed = jnp.swapaxes(by_frame, 0, 1)
    mixed = jnp.swapaxes(frame_block(framed, virt_attn, virtual, 2), 0, 1)
    return lax.all_to_all(mixed, ("track", "sub"), split_axis=0, concat_axis=1, tiled=True)


def solution(mesh):
    placed = (
        P(("groups", "track", "sub"), None, None),
        P(("groups", "track", "sub"), None),
        P(),
        P(),
        P(),
        P(),
        P(),
    )
    return jax.shard_map(
        shards,
        mesh=mesh,
        in_specs=placed,
        out_specs=P(("groups", "track", "sub"), None, None),
        check_vma=False,
    )
```

profile of v0, /device:TPU:0, one launch (start us, length us, event | category | flops | bytes accessed | tf_op | source)
XLA Modules:
  0.0 150.6 jit_solution(395790296589526434)
XLA Ops:
  0.0 1.3 copy.11.vis_ref
  1.3 31.1 %shard_map.73 = bf16[16,128,384]{2,1,0:T(8,128)(2,1)} custom-call(s32[16,2]{1,0:T(8,128)} %copy.11.vis_ref, bf16[16,128,384]{2,1,0:T(8,128)(2,1)} %tok_ref.1, bf16[4,384,384]{2,1,0:T(8,128)(2,1)} %attn_ref.2, bf16[384,1536]{1,0:T(8,128)(2,1)} %in_ref.1, bf16[1536,384]{1,0:T(8,128)(2,1)} %out_ref.1), custom_call_target="tpu_custom_call" | custom-call | tf_op jit(solution)/shard_map/pallas_call | solution.py:175
  32.4 2.3 %copy.12 = bf16[16,128,384]{2,0,1:T(8,128)(2,1)S(1)} copy(bf16[16,128,384]{2,1,0:T(8,128)(2,1)} %shard_map.73) | data formatting | bytes 3145728 | tf_op jit(solution)/shard_map/pallas_call | solution.py:175
  34.7 43.1 %all_to_all.36 = bf16[16,128,384]{2,0,1:T(8,128)(2,1)S(1)} all-to-all(bf16[16,128,384]{2,0,1:T(8,128)(2,1)S(1)} %copy.12), channel_id=1, replica_groups=mesh['groups'=2,'track'=8,'sub'=2] {'track','sub'}, dimensions={1} | all-to-all | bytes 3145728 | tf_op jit(solution)/shard_map/all_to_all | solution.py:206
  77.9 1.3 copy.13
  79.2 26.9 %shard_map.74 = bf16[8,256,384]{2,1,0:T(8,128)(2,1)} custom-call(bf16[8,256,384]{2,1,0:T(8,128)(2,1)} %bitcast.15, bf16[3,4,384,384]{3,2,1,0:T(8,128)(2,1)} %attn_ref.3, bf16[64,384]{1,0:T(8,128)(2,1)} %virtual_ref.1), custom_call_target="tpu_custom_call" | custom-call | tf_op jit(solution)/shard_map/pallas_call | solution.py:190
  106.1 2.3 %copy.14 = bf16[256,8,384]{2,1,0:T(8,128)(2,1)S(1)} copy(bf16[256,8,384]{2,0,1:T(8,128)(2,1)} %bitcast.16) | data formatting | bytes 3145728 | tf_op jit(solution)/shard_map/transpose | solution.py:208
  108.4 40.8 %all_to_all.37 = bf16[256,8,384]{2,1,0:T(8,128)(2,1)S(1)} all-to-all(bf16[256,8,384]{2,1,0:T(8,128)(2,1)S(1)} %copy.14), channel_id=1, replica_groups=mesh['groups'=2,'track'=8,'sub'=2] {'track','sub'}, dimensions={0} | all-to-all | bytes 3145728 | tf_op jit(solution)/shard_map/all_to_all | solution.py:209
  149.2 1.4 copy.17
where the time goes:
time: 151 us
  blocking collectives  83.9 us (56%)
  Pallas kernels  58 us (38%)
  local copies, waits for them, and re-layouts  8.69 us (6%)
    all_to_all x1, blocking collectives, shards(): lax.all_to_all(after, ('track', 'sub'), split_axis=1, concat_axis=0, tile...  43.1 us
    all_to_all x1, blocking collectives, shards(): lax.all_to_all(mixed, ('track', 'sub'), split_axis=0, concat_axis=1, tile...  40.8 us
    pallas_call x1, Pallas kernels, time_block(): pl.pallas_call(time_kernel, grid=(tracks // group,), in_specs=[pl.BlockSp...  31.1 us
    pallas_call x1, Pallas kernels, frame_block(): pl.pallas_call(frame_kernel, grid=(frames // group,), in_specs=[spec, WHO...  26.9 us

commit v1 on v0

--- a/solution.py
+++ b/solution.py
@@ -138,75 +138,162 @@
     return wide + project(jnp.concatenate(back, axis=0), attn_ref[2, 3])
 
 
-def time_kernel(vis_ref, tok_ref, attn_ref, in_ref, out_ref, x_ref, ones_ref):
+class Exchange:
+    def __init__(self, shape, slab_ref, dest_ref, send_sem, recv_sem, local_sem):
+        self.n_sub = shape["sub"]
+        self.count = shape["track"] * shape["sub"]
+        self.me = lax.axis_index("track") * self.n_sub + lax.axis_index("sub")
+        self.slab_ref, self.dest_ref = slab_ref, dest_ref
+        self.send_sem, self.recv_sem, self.local_sem = send_sem, recv_sem, local_sem
+        self.offsets = sorted(range(1, self.count), key=lambda j: abs(2 * j - self.count))
+
+    def device(self, peer):
+        return {"track": peer // self.n_sub, "sub": peer % self.n_sub}
+
+    def greet(self):
+        barrier = pltpu.get_barrier_semaphore()
+        for offset in self.offsets:
+            pl.semaphore_signal(
+                barrier,
+                inc=1,
+                device_id=self.device(lax.rem(self.me + offset, self.count)),
+                device_id_type=pl.DeviceIdType.MESH,
+            )
+
+    def admit(self):
+        pl.semaphore_wait(pltpu.get_barrier_semaphore(), self.count - 1)
+
+    def send(self, begin, rows):
+        each = self.slab_ref.shape[1]
+        target = self.dest_ref.at[pl.ds(self.me * each + begin, rows)]
+        for offset in self.offsets:
+            peer = lax.rem(self.me + offset, self.count)
+            pltpu.make_async_remote_copy(
+                src_ref=self.slab_ref.at[peer, pl.ds(begin, rows)],
+                dst_ref=target,
+                send_sem=self.send_sem,
+                recv_sem=self.recv_sem,
+                device_id=self.device(peer),
+                device_id_type=pl.DeviceIdType.MESH,
+            ).start()
+        pltpu.make_async_copy(self.slab_ref.at[self.me, pl.ds(begin, rows)], target, self.local_sem).start()
+
+    def finish(self):
+        each = self.slab_ref.shape[1]
+        others = self.dest_ref.at[pl.ds(0, (self.count - 1) * each)]
+        own = self.dest_ref.at[pl.ds(self.me * each, each)]
+        pltpu.make_async_copy(own, own, self.local_sem).wait()
+        pltpu.make_async_copy(others, others, self.send_sem).wait()
+        pltpu.make_async_copy(others, others, self.recv_sem).wait()
+
+
+def time_kernel(shape, vis_ref, tok_ref, attn_ref, in_ref, out_ref, dest_ref, ones_ref, slab_ref, *sems):
     step = pl.program_id(0)
     tracks, frames, feature = tok_ref.shape
+    exchange = Exchange(shape, slab_ref, dest_ref, *sems)
 
     @pl.when(step == 0)
     def _():
+        exchange.greet()
         fill_ones(ones_ref, feature)
 
     begin = [vis_ref[step * tracks + i, 0] for i in range(tracks)]
     end = [vis_ref[step * tracks + i, 1] for i in range(tracks)]
     after = time_step(tok_ref[...], begin, end, attn_ref, in_ref, out_ref, ones_ref)
-    x_ref[...] = after.astype(BF16).reshape(tracks, frames, feature)
-
-
-def frame_kernel(x_ref, attn_ref, virtual_ref, y_ref, query_ref, ones_ref):
+    for i in range(tracks):
+        block = after[i * frames : (i + 1) * frames].reshape(exchange.count, frames // exchange.count, feature)
+        slab_ref[:, step * tracks + i] = block.astype(BF16)
+
+    @pl.when(step == 0)
+    def _():
+        exchange.admit()
+
+    exchange.send(step * tracks, tracks)
+
+    @pl.when(step == pl.num_programs(0) - 1)
+    def _():
+        exchange.finish()
+
+
+def frame_kernel(shape, x_ref, attn_ref, virtual_ref, dest_ref, query_ref, ones_ref, slab_ref, *sems):
+    step = pl.program_id(0)
     frames, tracks, feature = x_ref.shape
-
-    @pl.when(pl.program_id(0) == 0)
-    def _():
+    exchange = Exchange(shape, slab_ref, dest_ref, *sems)
+
+    @pl.when(step == 0)
+    def _():
+        exchange.greet()
         fill_ones(ones_ref, feature)
         query = project(layer_norm(virtual_ref[...]), attn_ref[0, 0]).astype(BF16)
         query_ref[...] = spread_heads(query, head_masks(feature, BF16))
 
-    after = frame_step(x_ref[...], attn_ref, virtual_ref, query_ref, ones_ref)
-    y_ref[...] = after.astype(BF16).reshape(frames, tracks, feature)
+    after = frame_step(x_ref[...], attn_ref, virtual_ref, query_ref, ones_ref).astype(BF16)
+    for f in range(frames):
+        block = after[f * tracks : (f + 1) * tracks].reshape(exchange.count, tracks // exchange.count, feature)
+        slab_ref[:, step * frames + f] = block
+
+    @pl.when(step == 0)
+    def _():
+        exchange.admit()
+
+    exchange.send(step * frames, frames)
+
+    @pl.when(step == pl.num_programs(0) - 1)
+    def _():
+        exchange.finish()
 
 
 WHOLE = pl.BlockSpec(memory_space=pltpu.VMEM)
 LIMIT = 60 * 1024 * 1024
-
-
-def time_block(tokens, visible, time_attn, mlp_in, mlp_out, group):
+SEMS = [pltpu.SemaphoreType.DMA, pltpu.SemaphoreType.DMA, pltpu.SemaphoreType.DMA]
+
+
+def time_block(shape, tokens, visible, time_attn, mlp_in, mlp_out, group):
     tracks, frames, feature = tokens.shape
+    count = shape["track"] * shape["sub"]
+    each = frames // count
     spec = pl.BlockSpec((group, frames, feature), lambda i: (i, 0, 0))
     return pl.pallas_call(
-        time_kernel,
+        functools.partial(time_kernel, shape),
         grid=(tracks // group,),
         in_specs=[pl.BlockSpec(memory_space=pltpu.SMEM), spec, WHOLE, WHOLE, WHOLE],
-        out_specs=spec,
-        out_shape=jax.ShapeDtypeStruct(tokens.shape, BF16),
-        scratch_shapes=[pltpu.VMEM((HEADS * frames, feature), BF16)],
-        compiler_params=pltpu.CompilerParams(vmem_limit_bytes=LIMIT),
+        out_specs=pl.BlockSpec(memory_space=pl.ANY),
+        out_shape=jax.ShapeDtypeStruct((count * tracks, each, feature), BF16),
+        scratch_shapes=[
+            pltpu.VMEM((HEADS * frames, feature), BF16),
+            pltpu.VMEM((count, tracks, each, feature), BF16),
+        ]
+        + SEMS,
+        compiler_params=pltpu.CompilerParams(vmem_limit_bytes=LIMIT, collective_id=0, has_side_effects=True),
     )(visible, tokens, time_attn, mlp_in, mlp_out)
 
 
-def frame_block(framed, virt_attn, virtual, group):
+def frame_block(shape, framed, virt_attn, virtual, group):
     frames, tracks, feature = framed.shape
     n_virtual = virtual.shape[0]
+    count = shape["track"] * shape["sub"]
+    each = tracks // count
     spec = pl.BlockSpec((group, tracks, feature), lambda i: (i, 0, 0))
     return pl.pallas_call(
-        frame_kernel,
+        functools.partial(frame_kernel, shape),
         grid=(frames // group,),
         in_specs=[spec, WHOLE, WHOLE],
-        out_specs=spec,
-        out_shape=jax.ShapeDtypeStruct(framed.shape, BF16),
+        out_specs=pl.BlockSpec(memory_space=pl.ANY),
+        out_shape=jax.ShapeDtypeStruct((count * frames, each, feature), BF16),
         scratch_shapes=[
             pltpu.VMEM((HEADS * n_virtual, feature), BF16),
             pltpu.VMEM((HEADS * n_virtual, feature), BF16),
-        ],
-        compiler_params=pltpu.CompilerParams(vmem_limit_bytes=LIMIT),
+            pltpu.VMEM((count, frames, each, feature), BF16),
+        ]
+        + SEMS,
+        compiler_params=pltpu.CompilerParams(vmem_limit_bytes=LIMIT, collective_id=1, has_side_effects=True),
     )(framed, virt_attn, virtual)
 
 
-def shards(tokens, visible, time_attn, mlp_in, mlp_out, virt_attn, virtual):
-    after = time_block(tokens, visible, time_attn, mlp_in, mlp_out, 2)
-    by_frame = lax.all_to_all(after, ("track", "sub"), split_axis=1, concat_axis=0, tiled=True)
+def shards(shape, tokens, visible, time_attn, mlp_in, mlp_out, virt_attn, virtual):
+    by_frame = time_block(shape, tokens, visible, time_attn, mlp_in, mlp_out, 2)
     framed = jnp.swapaxes(by_frame, 0, 1)
-    mixed = jnp.swapaxes(frame_block(framed, virt_attn, virtual, 2), 0, 1)
-    return lax.all_to_all(mixed, ("track", "sub"), split_axis=0, concat_axis=1, tiled=True)
+    return jnp.swapaxes(frame_block(shape, framed, virt_attn, virtual, 2), 0, 1)
 
 
 def solution(mesh):
@@ -220,7 +307,7 @@
         P(),
     )
     return jax.shard_map(
-        shards,
+        functools.partial(shards, dict(mesh.shape)),
         mesh=mesh,
         in_specs=placed,
         out_specs=P(("groups", "track", "sub"), None, None),

time: 151 us -> 94.5 us (0.63)
  blocking collectives: 83.9 us -> 0 us
  Pallas kernels: 58 us -> 87.2 us
  local copies, waits for them, and re-layouts: 8.69 us -> 7.03 us
    all_to_all x2 -> x0, blocking collectives: 83.9 us -> none  [the longest x1 43.1 us: shards(): lax.all_to_all(after, ('track', 'sub'), split_axis=1, concat_axis=0, tile...]
    pallas_call x2, Pallas kernels: 58 us -> 87.2 us  [the longest x1 44.9 us: time_block(): pl.pallas_call(functools.partial(time_kernel, shape), grid=(tracks // gro...]
    all_to_all x2 -> x0, local copies, waits for them, and re-layouts: 2.69 us -> none  [the longest x1 1.39 us: shards(): lax.all_to_all(mixed, ('track', 'sub'), split_axis=0, concat_axis=1, tile...]
where the time goes in v1:
time: 94.5 us; the launch traced here: 94.3 us
  Pallas kernels  87.2 us (92%)
  local copies, waits for them, and re-layouts  7.03 us (7%)
    pallas_call x1, Pallas kernels, time_block(): pl.pallas_call(functools.partial(time_kernel, shape), grid=(tracks // gro...  44.9 us
    pallas_call x1, Pallas kernels, frame_block(): pl.pallas_call(functools.partial(frame_kernel, shape), grid=(frames // gr...  42.3 us
    transpose x1, local copies, waits for them, and re-layouts, shards(): return jnp.swapaxes(frame_block(shape, framed, virt_attn, virtual, 2), 0, 1)  2.92 us
    pallas_call x1, local copies, waits for them, and re-layouts, time_block(): pl.pallas_call(functools.partial(time_kernel, shape), grid=(tracks // gro...  2.75 us

profile of v1, /device:TPU:0, one launch (start us, length us, event | category | flops | bytes accessed | tf_op | source)
XLA Modules:
  0.0 94.3 jit_solution(7222722080391137361)
XLA Ops:
  0.0 1.4 %copy.8.vis_ref = s32[16,2]{1,0:T(8,128)} copy(s32[16,2]{0,1:T(2,128)} %param.8) | data formatting | bytes 256 | tf_op args[1]
  1.4 44.9 %shard_map.73 = bf16[256,8,384]{2,1,0:T(8,128)(2,1)} custom-call(s32[16,2]{1,0:T(8,128)} %copy.8.vis_ref, bf16[16,128,384]{2,1,0:T(8,128)(2,1)} %tok_ref.1, bf16[4,384,384]{2,1,0:T(8,128)(2,1)} %attn_ref.2, bf16[384,1536]{1,0:T(8,128)(2,1)} %in_ref.1, bf16[1536,384]{1,0:T(8,128)(2,1)} %out_ref.1), custom_call_target="tpu_custom_call" | custom-call | tf_op jit(solution)/shard_map/pallas_call | solution.py:256
  46.2 2.8 %copy.12 = bf16[256,8,384]{2,0,1:T(8,128)(2,1)} copy(bf16[256,8,384]{2,1,0:T(8,128)(2,1)} %shard_map.73) | data formatting | bytes 3145728 | tf_op jit(solution)/shard_map/pallas_call | solution.py:256
  49.0 42.3 %shard_map.74 = bf16[128,16,384]{2,1,0:T(8,128)(2,1)} custom-call(bf16[8,256,384]{2,1,0:T(8,128)(2,1)} %bitcast.4, bf16[3,4,384,384]{3,2,1,0:T(8,128)(2,1)} %attn_ref.3, bf16[64,384]{1,0:T(8,128)(2,1)} %virtual_ref.1), custom_call_target="tpu_custom_call" | custom-call | tf_op jit(solution)/shard_map/pallas_call | solution.py:277
  91.3 2.9 %copy.10 = bf16[16,128,384]{2,1,0:T(8,128)(2,1)} copy(bf16[16,128,384]{2,0,1:T(8,128)(2,1)} %bitcast.5) | data formatting | bytes 3145728 | tf_op jit(solution)/shard_map/transpose | solution.py:296

commit v2 on v0

--- a/solution.py
+++ b/solution.py
@@ -97,20 +97,15 @@
     return mixed.astype(BF16)
 
 
-def frame_step(framed, attn_ref, virtual_ref, query_ref, ones_ref):
-    frames, tracks, feature = framed.shape
+def frame_step(wide, key_c, value_c, query_b, attn_ref, virtual_ref, query_ref, ones_ref):
+    frames, tracks, feature = wide.shape
     n_virtual = virtual_ref.shape[0]
     scale = 1.0 / math.sqrt(feature // HEADS)
     masks = head_masks(feature, BF16)
     wide_masks = head_masks(feature, F32)
-    wide = framed.reshape(frames * tracks, feature).astype(F32)
-    normed = layer_norm(wide)
-    key_c = project(normed, attn_ref[0, 1]).astype(BF16)
-    value_c = project(normed, attn_ref[0, 2]).astype(BF16)
-    query_b = project(normed, attn_ref[2, 0]).astype(BF16)
-    track_part = [slice(f * tracks, (f + 1) * tracks) for f in range(frames)]
+    wide = wide.reshape(frames * tracks, feature).astype(F32)
     virtual_part = [slice(f * n_virtual, (f + 1) * n_virtual) for f in range(frames)]
-    cross = [few_queries(query_ref[...], key_c[part], value_c[part], wide_masks) for part in track_part]
+    cross = [few_queries(query_ref[...], key_c[f], value_c[f], wide_masks) for f in range(frames)]
     base = jnp.concatenate([virtual_ref[...].astype(F32)] * frames, axis=0)
     first = base + project(jnp.concatenate(cross, axis=0), attn_ref[0, 3])
     normed_w = layer_norm(first)
@@ -128,7 +123,7 @@
     back = []
     for frame in range(frames):
         part = virtual_part[frame]
-        scores = product(spread_heads(key_b[part], masks), query_b[track_part[frame]], 1, 1) * scale
+        scores = product(spread_heads(key_b[part], masks), query_b[frame], 1, 1) * scale
         scores = scores.reshape(HEADS, n_virtual, tracks)
         top = jnp.max(scores, axis=1, keepdims=True)
         weights = jnp.exp(scores - top).astype(BF16).reshape(HEADS * n_virtual, tracks)
@@ -138,75 +133,191 @@
     return wide + project(jnp.concatenate(back, axis=0), attn_ref[2, 3])
 
 
-def time_kernel(vis_ref, tok_ref, attn_ref, in_ref, out_ref, x_ref, ones_ref):
+class Exchange:
+    def __init__(self, shape):
+        self.n_sub = shape["sub"]
+        self.count = shape["track"] * shape["sub"]
+        self.me = lax.axis_index("track") * self.n_sub + lax.axis_index("sub")
+        self.offsets = sorted(range(1, self.count), key=lambda j: abs(2 * j - self.count))
+
+    def device(self, peer):
+        return {"track": peer // self.n_sub, "sub": peer % self.n_sub}
+
+    def greet(self):
+        barrier = pltpu.get_barrier_semaphore()
+        for offset in self.offsets:
+            pl.semaphore_signal(
+                barrier,
+                inc=1,
+                device_id=self.device(lax.rem(self.me + offset, self.count)),
+                device_id_type=pl.DeviceIdType.MESH,
+            )
+
+    def admit(self):
+        pl.semaphore_wait(pltpu.get_barrier_semaphore(), self.count - 1)
+
+    def send(self, source_of, target, send_sem, recv_sem, local_sem):
+        for offset in self.offsets:
+            peer = lax.rem(self.me + offset, self.count)
+            pltpu.make_async_remote_copy(
+                src_ref=source_of(peer),
+                dst_ref=target,
+                send_sem=send_sem,
+                recv_sem=recv_sem,
+                device_id=self.device(peer),
+                device_id_type=pl.DeviceIdType.MESH,
+            ).start()
+        pltpu.make_async_copy(source_of(self.me), target, local_sem).start()
+
+
+def await_bytes(ref, sem):
+    pltpu.make_async_copy(ref, ref, sem).wait()
+
+
+def layer_kernel(
+    shape, n_time, frame_group,
+    vis_ref, tok_ref, attn_ref, in_ref, out_ref, virt_hbm, virtual_ref, dest_ref,
+    time_ones, frame_ones, sort_ref, home_ref, query_ref, virt_ref,
+    slab, inbox, x_ref, key_ref, value_ref, qb_ref, outbox,
+    weight_sem, send1, recv1, local1, send2, recv2, local2,
+):
     step = pl.program_id(0)
-    tracks, frames, feature = tok_ref.shape
+    group, frames, feature = tok_ref.shape
+    exchange = Exchange(shape)
+    count = exchange.count
+    each = frames // count
+    chunk = count * group
+    tracks = chunk * n_time
+    own_tracks = n_time * group
+    lag = n_time // 2
+    frame_at = n_time + lag
 
     @pl.when(step == 0)
     def _():
-        fill_ones(ones_ref, feature)
-
-    begin = [vis_ref[step * tracks + i, 0] for i in range(tracks)]
-    end = [vis_ref[step * tracks + i, 1] for i in range(tracks)]
-    after = time_step(tok_ref[...], begin, end, attn_ref, in_ref, out_ref, ones_ref)
-    x_ref[...] = after.astype(BF16).reshape(tracks, frames, feature)
-
-
-def frame_kernel(x_ref, attn_ref, virtual_ref, y_ref, query_ref, ones_ref):
-    frames, tracks, feature = x_ref.shape
-
-    @pl.when(pl.program_id(0) == 0)
-    def _():
-        fill_ones(ones_ref, feature)
-        query = project(layer_norm(virtual_ref[...]), attn_ref[0, 0]).astype(BF16)
+        exchange.greet()
+        pltpu.make_async_copy(virt_hbm, virt_ref, weight_sem).start()
+        fill_ones(time_ones, feature)
+
+    @pl.when(step < n_time)
+    def _():
+        begin = [vis_ref[0, step * group + i] for i in range(group)]
+        end = [vis_ref[1, step * group + i] for i in range(group)]
+        after = time_step(tok_ref[...], begin, end, attn_ref, in_ref, out_ref, time_ones)
+        for i in range(group):
+            block = after[i * frames : (i + 1) * frames].reshape(count, each, feature)
+            slab[step, :, i] = block.astype(BF16)
+
+        @pl.when(step == 0)
+        def _():
+            exchange.admit()
+
+        exchange.send(
+            lambda peer: slab.at[step, peer], inbox.at[step, exchange.me], send1, recv1.at[step], local1.at[step]
+        )
+
+    @pl.when(step == lag)
+    def _():
+        pltpu.make_async_copy(virt_hbm, virt_ref, weight_sem).wait()
+        fill_ones(frame_ones, feature)
+        query = project(layer_norm(virtual_ref[...]), virt_ref[0, 0]).astype(BF16)
         query_ref[...] = spread_heads(query, head_masks(feature, BF16))
-
-    after = frame_step(x_ref[...], attn_ref, virtual_ref, query_ref, ones_ref)
-    y_ref[...] = after.astype(BF16).reshape(frames, tracks, feature)
+        row = lax.broadcasted_iota(jnp.int32, (chunk * each, chunk * each), 0)
+        col = lax.broadcasted_iota(jnp.int32, (chunk * each, chunk * each), 1)
+        sort_ref[...] = jnp.where(col == row % chunk * each + row // chunk, 1.0, 0.0).astype(BF16)
+        row = lax.broadcasted_iota(jnp.int32, (tracks, tracks), 0)
+        col = lax.broadcasted_iota(jnp.int32, (tracks, tracks), 1)
+        track = row % own_tracks
+        place = track // group * chunk + row // own_tracks * group + track % group
+        home_ref[...] = jnp.where(col == place, 1.0, 0.0).astype(BF16)
+
+    def arrive(index):
+        await_bytes(inbox.at[index, pl.ds(0, count - 1)], recv1.at[index])
+        await_bytes(inbox.at[index, 0], local1.at[index])
+        rows = inbox[index].reshape(chunk * each, feature)
+        rows = project(sort_ref[...], rows).astype(BF16)
+        normed = layer_norm(rows)
+        place = pl.ds(pl.multiple_of(index * chunk, chunk), chunk)
+        for ref, values in (
+            (x_ref, rows),
+            (key_ref, project(normed, virt_ref[0, 1]).astype(BF16)),
+            (value_ref, project(normed, virt_ref[0, 2]).astype(BF16)),
+            (qb_ref, project(normed, virt_ref[2, 0]).astype(BF16)),
+        ):
+            ref[:, place] = values.reshape(each, chunk, feature)
+
+    @pl.when((step >= lag) & (step < frame_at))
+    def _():
+        arrive(step - lag)
+
+    @pl.when(step >= frame_at)
+    def _():
+        first = (step - frame_at) * frame_group
+        part = pl.ds(first, frame_group)
+        after = frame_step(
+            x_ref[part], key_ref[part], value_ref[part], qb_ref[part], virt_ref, virtual_ref, query_ref, frame_ones
+        ).astype(BF16)
+        for f in range(frame_group):
+            block = project(home_ref[...], after[f * tracks : (f + 1) * tracks]).astype(BF16)
+            outbox[:, first + f] = block.reshape(count, own_tracks, feature)
+        exchange.send(
+            lambda peer: outbox.at[peer, part],
+            dest_ref.at[pl.ds(exchange.me * each + first, frame_group)],
+            send2,
+            recv2,
+            local2,
+        )
+
+    @pl.when(step == pl.num_programs(0) - 1)
+    def _():
+        await_bytes(slab.at[:, pl.ds(0, count - 1)], send1)
+        others = dest_ref.at[pl.ds(0, (count - 1) * each)]
+        await_bytes(dest_ref.at[pl.ds(0, each)], local2)
+        await_bytes(others, send2)
+        await_bytes(others, recv2)
 
 
 WHOLE = pl.BlockSpec(memory_space=pltpu.VMEM)
+ANY = pl.BlockSpec(memory_space=pl.ANY)
 LIMIT = 60 * 1024 * 1024
 
 
-def time_block(tokens, visible, time_attn, mlp_in, mlp_out, group):
-    tracks, frames, feature = tokens.shape
-    spec = pl.BlockSpec((group, frames, feature), lambda i: (i, 0, 0))
-    return pl.pallas_call(
-        time_kernel,
-        grid=(tracks // group,),
-        in_specs=[pl.BlockSpec(memory_space=pltpu.SMEM), spec, WHOLE, WHOLE, WHOLE],
-        out_specs=spec,
-        out_shape=jax.ShapeDtypeStruct(tokens.shape, BF16),
-        scratch_shapes=[pltpu.VMEM((HEADS * frames, feature), BF16)],
-        compiler_params=pltpu.CompilerParams(vmem_limit_bytes=LIMIT),
-    )(visible, tokens, time_attn, mlp_in, mlp_out)
-
-
-def frame_block(framed, virt_attn, virtual, group):
-    frames, tracks, feature = framed.shape
+def shards(shape, tokens, visible, time_attn, mlp_in, mlp_out, virt_attn, virtual):
+    own_tracks, frames, feature = tokens.shape
     n_virtual = virtual.shape[0]
-    spec = pl.BlockSpec((group, tracks, feature), lambda i: (i, 0, 0))
-    return pl.pallas_call(
-        frame_kernel,
-        grid=(frames // group,),
-        in_specs=[spec, WHOLE, WHOLE],
-        out_specs=spec,
-        out_shape=jax.ShapeDtypeStruct(framed.shape, BF16),
+    count = shape["track"] * shape["sub"]
+    group, frame_group = 2, 2
+    each = frames // count
+    n_time = own_tracks // group
+    tracks = count * own_tracks
+    chunk = count * group
+    by_frame = pltpu.VMEM((each, tracks, feature), BF16)
+    dma = pltpu.SemaphoreType.DMA
+    result = pl.pallas_call(
+        functools.partial(layer_kernel, shape, n_time, frame_group),
+        grid=(n_time + n_time // 2 + each // frame_group,),
+        in_specs=[
+            pl.BlockSpec(memory_space=pltpu.SMEM),
+            pl.BlockSpec((group, frames, feature), lambda i: (jnp.minimum(i, n_time - 1), 0, 0)),
+            WHOLE, WHOLE, WHOLE, ANY, WHOLE,
+        ],
+        out_specs=ANY,
+        out_shape=jax.ShapeDtypeStruct((frames, own_tracks, feature), BF16),
         scratch_shapes=[
+            pltpu.VMEM((HEADS * frames, feature), BF16),
             pltpu.VMEM((HEADS * n_virtual, feature), BF16),
+            pltpu.VMEM((chunk * each, chunk * each), BF16),
+            pltpu.VMEM((tracks, tracks), BF16),
             pltpu.VMEM((HEADS * n_virtual, feature), BF16),
+            pltpu.VMEM(virt_attn.shape, BF16),
+            pltpu.VMEM((n_time, count, group, each, feature), BF16),
+            pltpu.VMEM((n_time, count, group, each, feature), BF16),
+            by_frame, by_frame, by_frame, by_frame,
+            pltpu.VMEM((count, each, own_tracks, feature), BF16),
+            dma, dma, dma((n_time,)), dma((n_time,)), dma, dma, dma,
         ],
-        compiler_params=pltpu.CompilerParams(vmem_limit_bytes=LIMIT),
-    )(framed, virt_attn, virtual)
-
-
-def shards(tokens, visible, time_attn, mlp_in, mlp_out, virt_attn, virtual):
-    after = time_block(tokens, visible, time_attn, mlp_in, mlp_out, 2)
-    by_frame = lax.all_to_all(after, ("track", "sub"), split_axis=1, concat_axis=0, tiled=True)
-    framed = jnp.swapaxes(by_frame, 0, 1)
-    mixed = jnp.swapaxes(frame_block(framed, virt_attn, virtual, 2), 0, 1)
-    return lax.all_to_all(mixed, ("track", "sub"), split_axis=0, concat_axis=1, tiled=True)
+        compiler_params=pltpu.CompilerParams(vmem_limit_bytes=LIMIT, collective_id=0, has_side_effects=True),
+    )(visible.T, tokens, time_attn, mlp_in, mlp_out, virt_attn, virtual)
+    return jnp.swapaxes(result, 0, 1)
 
 
 def solution(mesh):
@@ -220,7 +331,7 @@
         P(),
     )
     return jax.shard_map(
-        shards,
+        functools.partial(shards, dict(mesh.shape)),
         mesh=mesh,
         in_specs=placed,
         out_specs=P(("groups", "track", "sub"), None, None),

time: 151 us -> 88.9 us (0.59)
  blocking collectives: 83.9 us -> 0 us
  Pallas kernels: 58 us -> 85.8 us
  local copies, waits for them, and re-layouts: 8.69 us -> 2.92 us
    all_to_all x2 -> x0, blocking collectives: 83.9 us -> none  [the longest x1 43.1 us: shards(): lax.all_to_all(after, ('track', 'sub'), split_axis=1, concat_axis=0, tile...]
    pallas_call x2 -> x1, Pallas kernels: 58 us -> 85.8 us  [shards(): pl.pallas_call(functools.partial(layer_kernel, shape, n_time, frame_group...]
    all_to_all x2 -> x0, local copies, waits for them, and re-layouts: 2.69 us -> none  [the longest x1 1.39 us: shards(): lax.all_to_all(mixed, ('track', 'sub'), split_axis=0, concat_axis=1, tile...]
    pallas_call x1 -> x0, local copies, waits for them, and re-layouts: 2.33 us -> none  [time_block(): pl.pallas_call(time_kernel, grid=(tracks // group,), in_specs=[pl.BlockSp...]
where the time goes in v2:
time: 88.9 us; the launch traced here: 88.7 us
  Pallas kernels  85.8 us (97%)
  local copies, waits for them, and re-layouts  2.92 us (3%)
    pallas_call x1, Pallas kernels, shards(): pl.pallas_call(functools.partial(layer_kernel, shape, n_time, frame_group...  85.8 us
    transpose x1, local copies, waits for them, and re-layouts, shards(): return jnp.swapaxes(result, 0, 1)  2.92 us

profile of v2, /device:TPU:0, one launch (start us, length us, event | category | flops | bytes accessed | tf_op | source)
XLA Modules:
  0.0 88.7 jit_solution(11339492784810561630)
XLA Ops:
  0.0 85.8 %shard_map.73 = bf16[128,16,384]{2,1,0:T(8,128)(2,1)} custom-call(s32[2,16]{1,0:T(2,128)} %bitcast.3, bf16[16,128,384]{2,1,0:T(8,128)(2,1)} %tok_ref.1, bf16[4,384,384]{2,1,0:T(8,128)(2,1)} %attn_ref.1, bf16[384,1536]{1,0:T(8,128)(2,1)} %in_ref.1, bf16[1536,384]{1,0:T(8,128)(2,1)} %out_ref.1, bf16[3,4,384,384]{3,2,1,0:T(8,128)(2,1)} %virt_hbm.1, ...), custom_call_target="tpu_custom_call" | custom-call | tf_op jit(solution)/shard_map/pallas_call | solution.py:295
  85.8 2.9 %copy.8 = bf16[16,128,384]{2,1,0:T(8,128)(2,1)} copy(bf16[16,128,384]{2,0,1:T(8,128)(2,1)} %bitcast.2) | data formatting | bytes 3145728 | tf_op jit(solution)/shard_map/transpose | solution.py:320
